TPU v7x, 32 devices: a whole 2x2x4 slice. The times are simulated.
32 devices in a mesh: grp: 4 (over x, core), blk: 8 (over z, y).
Axes of the slice: x: 2, y: 2, z: 4, core: 2. Of those that a mesh axis runs over, the one named last changes fastest.
Arguments:
- vector: bfloat16 [32, 128], P(('grp', 'blk')), may hold values from -6 to 6
- integrals: bfloat16 [1024, 500, 500], P(('grp', 'blk')), may hold values from -0.072 to 0.072
- orbitals: bfloat16 [26, 500], replicated, may hold values from -0.25 to 0.25
- alpha_addr: int32 [32, 676], replicated, may hold values from 0 to 31
- alpha_sign: int32 [32, 676], replicated, may hold values from -1 to 1
- beta_addr: int32 [128, 676], replicated, may hold values from 0 to 127
- beta_sign: int32 [128, 676], replicated, may hold values from -1 to 1
- seg_alpha: int32 [32], replicated, may hold values from 0 to 9, never falling along the last dimension, each value on 1 to 6 neighbouring positions
- seg_beta: int32 [128], replicated, may hold values from 0 to 9, never falling along the last dimension, each value on 1 to 25 neighbouring positions
- allowed: int32 [10, 10], replicated, may hold values 0 or 1
Outputs:
- sigma_t: float32 [128, 32], P(('grp', 'blk'))
All inputs are finite; a program needn't handle non-finite values.
Results may differ from a plain program's by a relative error of at most 0.0056.
Values may be sent and summed in bfloat16 or wider, within the bound.
No kernel may reach another device: no remote copies, remote signals or barrier semaphores. Data moves between devices by JAX's collectives and lax.ppermute only.
A program may use at most 64 MiB of HBM per device.

v0:
```python
import functools

import jax
import jax.numpy as jnp
from jax import lax
from jax.experimental import pallas as pl
from jax.experimental.pallas import tpu as pltpu
from jax.sharding import PartitionSpec as P


AXES = ("grp", "blk")
LANES = 128
SUBLANES = 8
PACK = 16
UNROLL = 672
AHEAD = 3
HEAD = 25
BLOCK = 50
PREPARE_AT = 1
VMEM_LIMIT = 32 * 2**20
WIDE_LIMIT = 50 * 2**20
NT = (((1,), (1,)), ((), ()))
TN = (((0,), (0,)), ((), ()))


def placed_rows(values, before, total):
    width = values.shape[1]
    pieces = [jnp.zeros((before, width), values.dtype)] if before else []
    pieces.append(values)
    after = total - before - values.shape[0]
    if after:
        pieces.append(jnp.zeros((after, width), values.dtype))
    return jnp.concatenate(pieces, axis=0) if len(pieces) > 1 else values


def prepare(addr_ref, sign_ref, seg_a_ref, seg_b_ref, allowed_ref, hot_ref, mask_ref):
    side, rows, _ = hot_ref.shape
    halves, held, n_beta = mask_ref.shape
    n_alpha = addr_ref.shape[0]
    blocks = allowed_ref.shape[0]
    base = lax.axis_index("grp") % halves * held
    addr = addr_ref[...] - base
    sign = sign_ref[...].astype(jnp.float32)
    for q in range(side):
        for g in range(rows // n_alpha):
            hot_ref[q, g * n_alpha : (g + 1) * n_alpha, :] = jnp.where(addr == g * side + q, sign, 0.0).astype(
                jnp.bfloat16
            )
    hot_b = (lax.broadcasted_iota(jnp.int32, (blocks, n_beta), 0) == seg_b_ref[...]).astype(jnp.float32)
    hot_a = (lax.broadcasted_iota(jnp.int32, (blocks, n_alpha), 0) == seg_a_ref[...]).astype(jnp.float32)
    columns = jnp.dot(allowed_ref[...].astype(jnp.float32), hot_b, preferred_element_type=jnp.float32)
    mask_ref[...] = lax.dot_general(hot_a, columns, TN, preferred_element_type=jnp.float32).reshape(
        halves, held, n_beta
    )


def start_kernel(vector_any, big_ref, out_any, head_ref, vector_ref, copy_ref, sem):
    size = head_ref.shape[1]
    vector = pltpu.make_async_copy(vector_any, vector_ref, sem.at[0])
    head = [
        pltpu.make_async_copy(
            big_ref.at[pl.ds(part * (big_ref.shape[0] // 2), size)], head_ref.at[part], sem.at[1 + part]
        )
        for part in range(2)
    ]
    out = pltpu.make_async_copy(copy_ref, out_any, sem.at[3])
    vector.start()
    for copy in head:
        copy.start()
    vector.wait()
    copy_ref[...] = jnp.broadcast_to(vector_ref[...][None], copy_ref.shape)
    out.start()
    out.wait()
    for copy in head:
        copy.wait()


def start(vector, integrals, devices):
    aux, nbas, _ = integrals.shape
    if not fits(integrals):
        return jnp.broadcast_to(vector, (devices,) + vector.shape), None
    hbm = pl.BlockSpec(memory_space=pltpu.HBM)
    vector, turned = (
        pltpu.with_memory_space_constraint(t, pltpu.HBM) for t in (vector, jnp.transpose(integrals, (1, 0, 2)))
    )
    return pl.pallas_call(
        start_kernel,
        in_specs=[hbm] * 2,
        out_specs=(hbm, pl.BlockSpec(memory_space=pltpu.VMEM)),
        out_shape=(
            jax.ShapeDtypeStruct((devices,) + vector.shape, vector.dtype),
            jax.ShapeDtypeStruct((2, min(HEAD, nbas // 2), aux, nbas), integrals.dtype),
        ),
        scratch_shapes=[
            pltpu.VMEM(vector.shape, vector.dtype),
            pltpu.VMEM((devices,) + vector.shape, vector.dtype),
            pltpu.SemaphoreType.DMA((4,)),
        ],
        compiler_params=pltpu.CompilerParams(vmem_limit_bytes=VMEM_LIMIT),
        name="start",
    )(vector, turned)


def fits(integrals):
    aux, nbas, _ = integrals.shape
    return aux % PACK == 0 and aux // PACK * 64 == LANES and nbas % 2 == 0


def transform_kernel(
    big_ref,
    head_ref,
    orb_any,
    addr_any,
    sign_any,
    seg_a_any,
    seg_b_any,
    allowed_any,
    out_ref,
    hot_ref,
    mask_ref,
    block_ref,
    orb_ref,
    addr_ref,
    sign_ref,
    seg_a_ref,
    seg_b_ref,
    allowed_ref,
    half_ref,
    turn_ref,
    big_sem,
    small_sem,
    *,
    sizes,
    half,
    stride,
):
    norb, nbas = orb_ref.shape
    groups = big_ref.shape[1] // PACK
    starts = [sum(sizes[:s]) for s in range(len(sizes))]
    first = head_ref.shape[1]

    def fetch(s):
        return [
            pltpu.make_async_copy(
                big_ref.at[pl.ds(part * half + starts[s], sizes[s])],
                block_ref.at[part, pl.ds(starts[s] - first, sizes[s])],
                big_sem.at[s, part],
            )
            for part in range(2)
        ]

    small = [
        pltpu.make_async_copy(a, b, small_sem.at[k])
        for k, (a, b) in enumerate(
            (
                (orb_any, orb_ref),
                (addr_any, addr_ref),
                (sign_any, sign_ref),
                (seg_a_any, seg_a_ref),
                (seg_b_any, seg_b_ref),
                (allowed_any, allowed_ref),
            )
        )
    ]
    for copy in small:
        copy.start()
    for s in range(1, 1 + AHEAD):
        for copy in fetch(s):
            copy.start()
    small[0].wait()
    weights = orb_ref[...]
    for s, size in enumerate(sizes):
        source, begin = (block_ref, starts[s] - first) if s else (head_ref, 0)
        for copy in fetch(s) if s else ():
            copy.wait()
        if 0 < s < len(sizes) - AHEAD:
            for copy in fetch(s + AHEAD):
                copy.start()
        cuts = [0, size // 2, size]
        total = [None, None]
        for part in range(2):
            for group in range(groups):
                placed = placed_rows(weights, (part * groups + group) * 32, LANES)
                for k in range(2):
                    block = source[
                        part,
                        begin + cuts[k] : begin + cuts[k + 1],
                        group * PACK : (group + 1) * PACK,
                        :,
                    ].reshape(-1, nbas)
                    piece = lax.dot_general(block, placed, NT, preferred_element_type=jnp.float32)
                    total[k] = piece if total[k] is None else total[k] + piece
        for k in range(2):
            for row in range(cuts[k + 1] - cuts[k]):
                half_ref[pl.ds(starts[s] + cuts[k] + row, PACK, stride=stride), :] = total[k][
                    row * PACK : (row + 1) * PACK, :
                ]
        if s == PREPARE_AT:
            for copy in small[1:]:
                copy.wait()
            prepare(addr_ref, sign_ref, seg_a_ref, seg_b_ref, allowed_ref, hot_ref, mask_ref)
    both = jnp.concatenate(
        [placed_rows(weights[:, part * half : (part + 1) * half], 0, 32) for part in range(2)], axis=0
    )
    for r in range(PACK):
        right = half_ref[r * stride : r * stride + half, :].astype(jnp.bfloat16)
        sums = jnp.dot(both, right, preferred_element_type=jnp.float32)
        turn_ref[pl.ds(r, norb, stride=PACK), :] = sums[:norb] + pltpu.roll(sums[32 : 32 + norb], LANES - groups * 32, 1)
    flatten(turn_ref, out_ref, norb, groups)


def flatten(turn_ref, out_ref, norb, groups):
    lane = lax.broadcasted_iota(jnp.int32, (PACK, LANES), 1)
    pairs = norb * norb
    tiles = -(-(pairs + (groups - 1) * 32) // LANES)
    value = [[jnp.zeros((PACK, LANES), jnp.float32) for _ in range(tiles)] for _ in range(groups)]
    for i in range(norb):
        moved = pltpu.roll(turn_ref[i * PACK : (i + 1) * PACK, :], i * norb % LANES, 1)
        for group in range(groups):
            begin = i * norb + group * 32
            for tile in range(begin // LANES, (begin + norb - 1) // LANES + 1):
                low = begin - tile * LANES
                keep = (lane >= low) & (lane < low + norb)
                value[group][tile] = jnp.where(keep, moved, value[group][tile])
    for group in range(groups):
        shift = group * 32
        for tile in range(-(-pairs // LANES)):
            ends = min(LANES, pairs - tile * LANES)
            result = value[group][tile]
            if shift:
                result = pltpu.roll(result, LANES - shift, 1)
                if tile + 1 < tiles:
                    result = jnp.where(
                        lane < LANES - shift, result, pltpu.roll(value[group][tile + 1], LANES - shift, 1)
                    )
            out_ref[group * PACK : (group + 1) * PACK, tile * LANES : tile * LANES + ends] = result[:, :ends].astype(
                jnp.bfloat16
            )


def transform(integrals, head, orbitals, tables, hot_shape, mask_shape):
    aux, nbas, _ = integrals.shape
    norb = orbitals.shape[0]
    half = nbas // 2
    made = (jax.ShapeDtypeStruct(hot_shape, jnp.bfloat16), jax.ShapeDtypeStruct(mask_shape, jnp.float32))
    if head is None:
        half_done = jnp.einsum("jn,pmn->pjm", orbitals, integrals, preferred_element_type=jnp.float32).astype(
            jnp.bfloat16
        )
        factors = (
            jnp.einsum("im,pjm->pij", orbitals, half_done, preferred_element_type=jnp.float32)
            .reshape(aux, norb * norb)
            .astype(jnp.bfloat16)
        )
        return factors, *pl.pallas_call(prepare, out_shape=made, name="prepare")(*tables)
    sizes = (head.shape[1],) + block_sizes(half - head.shape[1])
    stride = -(-half // 4) * 4
    stride += 4 if stride % SUBLANES == 0 else 0
    hbm = pl.BlockSpec(memory_space=pltpu.HBM)
    turned = jnp.transpose(integrals, (1, 0, 2))
    turned, orbitals, *tables = (
        pltpu.with_memory_space_constraint(t, pltpu.HBM) for t in (turned, orbitals, *tables)
    )
    return pl.pallas_call(
        functools.partial(transform_kernel, sizes=sizes, half=half, stride=stride),
        in_specs=[hbm, pl.BlockSpec(memory_space=pltpu.VMEM)] + [hbm] * (1 + len(tables)),
        out_shape=(jax.ShapeDtypeStruct((aux, norb * norb), jnp.bfloat16),) + made,
        scratch_shapes=[
            pltpu.VMEM((2, half - sizes[0], aux, nbas), jnp.bfloat16),
            pltpu.VMEM(orbitals.shape, orbitals.dtype),
        ]
        + [pltpu.VMEM(t.shape, t.dtype) for t in tables]
        + [
            pltpu.VMEM((PACK * stride, LANES), jnp.float32),
            pltpu.VMEM((norb * PACK, LANES), jnp.float32),
            pltpu.SemaphoreType.DMA((len(sizes), 2)),
            pltpu.SemaphoreType.DMA((1 + len(tables),)),
        ],
        cost_estimate=pl.CostEstimate(
            flops=4 * aux * nbas * nbas * LANES, transcendentals=0, bytes_accessed=2 * aux * nbas * nbas
        ),
        compiler_params=pltpu.CompilerParams(vmem_limit_bytes=WIDE_LIMIT),
        name="transform",
    )(turned, head, orbitals, *tables)


def block_sizes(rows):
    sizes, left = [], rows
    while left:
        size = min(left, BLOCK if left > BLOCK else BLOCK // 2)
        sizes.append(size)
        left -= size
    return tuple(sizes)


def split(value):
    high = value.astype(jnp.bfloat16)
    return high, (value - high.astype(jnp.float32)).astype(jnp.bfloat16)


def set_sources(vec_ref, mask_ref, source_ref):
    halves, mine, _ = mask_ref.shape
    held = source_ref.shape[1]
    core = lax.axis_index("grp") % halves
    for k in range(mine):
        source_ref[k // held, k % held : k % held + 1, :] = (
            vec_ref[core * mine + k].astype(jnp.float32) * mask_ref[core, k : k + 1, :]
        )


def gather_pairs(turn, addr_ref, sign_ref, source_ref, pairs_ref):
    pairs, n_beta = addr_ref.shape
    held = source_ref.shape[1]
    chunks = n_beta // LANES

    def gathered(k, index):
        value = None
        for c in range(chunks):
            row = jnp.broadcast_to(
                source_ref[turn, k : k + 1, c * LANES : (c + 1) * LANES], (index.shape[0], LANES)
            )
            found = jnp.take_along_axis(row, index % LANES if chunks > 1 else index, axis=1, mode="promise_in_bounds")
            value = found if value is None else jnp.where(index // LANES == c, found, value)
        return value

    def fill(start, count):
        for c in range(chunks):
            index = addr_ref[pl.ds(start, count), c * LANES : (c + 1) * LANES]
            sign = sign_ref[pl.ds(start, count), c * LANES : (c + 1) * LANES].astype(jnp.float32)
            for k in range(held):
                place = k * n_beta + c * LANES
                pairs_ref[pl.ds(start, count), place : place + LANES] = (gathered(k, index) * sign).astype(jnp.bfloat16)

    together = pairs // SUBLANES
    unroll = max(
        u for u in range(1, together + 1) if together % u == 0 and (u == 1 or u * held * chunks**2 <= UNROLL)
    )

    def step(i, carry):
        for u in range(unroll):
            fill(pl.multiple_of((i * unroll + u) * SUBLANES, SUBLANES), SUBLANES)
        return carry

    lax.fori_loop(0, together // unroll, step, 0)
    if pairs % SUBLANES:
        fill(together * SUBLANES, pairs % SUBLANES)


def set_alpha(factors, hot_ref, h_ref):
    side = hot_ref.shape[0]
    n_alpha, width = h_ref.shape
    total = None
    for q in range(side):
        part = lax.dot_general(
            hot_ref[q],
            placed_rows(factors, q * factors.shape[0], LANES),
            NT,
            preferred_element_type=jnp.float32,
        )
        total = part if total is None else total + part
    for g in range(width // LANES):
        h_ref[:, g * LANES : (g + 1) * LANES] = total[g * n_alpha : (g + 1) * n_alpha, :]


def contract_pairs(turn, factors, pairs_ref, t_ref, n_beta):
    aux, pairs = factors.shape
    held = t_ref.shape[1] // aux
    wide = max(1, 256 // n_beta)
    for first in range(0, held, wide):
        last = min(first + wide, held)
        part = jnp.dot(factors, pairs_ref[:pairs, first * n_beta : last * n_beta], preferred_element_type=jnp.float32)
        for k in range(first, last):
            t_ref[turn, k * aux : (k + 1) * aux, :] = part[:, (k - first) * n_beta : (k - first + 1) * n_beta]


def finish(h_ref, t_ref, mask_ref, turn_ref, out_ref):
    n_alpha, width = h_ref.shape
    n_beta = mask_ref.shape[2]
    h_high, h_low = split(h_ref[...])
    t_high, t_low = split(t_ref[...].reshape(width, n_beta))
    both = jnp.dot(jnp.concatenate([h_high, h_low], axis=0), t_high, preferred_element_type=jnp.float32)
    rest = jnp.dot(h_high, t_low, preferred_element_type=jnp.float32)
    partial = both[:n_alpha] + (both[n_alpha:] + rest)
    turn_ref[...] = (partial * mask_ref[...].reshape(n_alpha, n_beta)).T
    devices = out_ref.shape[0]
    local = n_beta // devices
    out_ref[...] = jnp.concatenate(
        [turn_ref[pl.ds(k, devices, stride=local), :] for k in range(local)], axis=1
    )


def gather_kernel(vec_ref, mask_ref, addr_ref, sign_ref, pairs_ref, source_ref):
    set_sources(vec_ref, mask_ref, source_ref)
    gather_pairs(0, addr_ref, sign_ref, source_ref, pairs_ref)


def contract_kernel(own_ref, other_ref, hot_ref, mask_ref, pairs_ref, out_ref, h_ref, t_ref, turn_ref):
    factors = jnp.concatenate([own_ref[...], other_ref[...]], axis=0)
    set_alpha(factors, hot_ref, h_ref)
    contract_pairs(0, factors, pairs_ref, t_ref, mask_ref.shape[2])
    finish(h_ref, t_ref, mask_ref, turn_ref, out_ref)


def beta_kernel(
    vec_ref,
    own_ref,
    other_ref,
    hot_ref,
    mask_ref,
    addr_ref,
    sign_ref,
    out_ref,
    source_ref,
    pairs_ref,
    h_ref,
    t_ref,
    turn_ref,
):
    set_sources(vec_ref, mask_ref, source_ref)
    factors = jnp.concatenate([own_ref[...], other_ref[...]], axis=0)
    set_alpha(factors, hot_ref, h_ref)

    @pl.loop(0, source_ref.shape[0])
    def _(turn):
        gather_pairs(turn, addr_ref, sign_ref, source_ref, pairs_ref)
        contract_pairs(turn, factors, pairs_ref, t_ref, mask_ref.shape[2])

    finish(h_ref, t_ref, mask_ref, turn_ref, out_ref)


def beta_side(vec, own, hot, mask, beta_addr, beta_sign, devices):
    aux, pairs = own.shape
    halves, mine, n_beta = mask.shape
    groups = lax.axis_size("grp")
    other = lax.ppermute(own, "grp", [(g, g ^ 1) for g in range(groups)])
    addr, sign = beta_addr.T, beta_sign.T
    held = max(k for k in range(1, mine + 1) if mine % k == 0 and k * pairs * n_beta * 2 <= 12 * 2**20)
    params = pltpu.CompilerParams(vmem_limit_bytes=VMEM_LIMIT)
    made = jax.ShapeDtypeStruct((devices, n_beta // devices * halves * mine), jnp.float32)
    source = pltpu.VMEM((mine // held, held, n_beta), jnp.float32)
    product = jax.ShapeDtypeStruct((pairs, held * n_beta), jnp.bfloat16)
    sums = [
        pltpu.VMEM((halves * mine, mine * 2 * aux), jnp.float32),
        pltpu.VMEM((mine // held, held * 2 * aux, n_beta), jnp.float32),
        pltpu.VMEM((n_beta, halves * mine), jnp.float32),
    ]
    if held == mine:
        terms = pl.pallas_call(
            gather_kernel,
            out_shape=product,
            scratch_shapes=[source],
            compiler_params=params,
            cost_estimate=pl.CostEstimate(flops=0, transcendentals=0, bytes_accessed=8 * pairs * mine * n_beta),
            name="gather",
        )(vec, mask, addr, sign)
        return pl.pallas_call(
            contract_kernel, out_shape=made, scratch_shapes=sums, compiler_params=params, name="contract"
        )(own, other, hot, mask, terms)
    return pl.pallas_call(
        beta_kernel,
        out_shape=made,
        scratch_shapes=[source, pltpu.VMEM(product.shape, product.dtype)] + sums,
        compiler_params=params,
        name="beta_side",
    )(vec, own, other, hot, mask, addr, sign)


def add_kernel(parts_ref, out_ref):
    total = jnp.sum(parts_ref[...], axis=0, keepdims=True)
    rows, columns = out_ref.shape
    for k in range(rows):
        out_ref[k : k + 1, :] = total[:, k * columns : (k + 1) * columns]


def on_device(
    vector,
    integrals,
    orbitals,
    alpha_addr,
    alpha_sign,
    beta_addr,
    beta_sign,
    seg_alpha,
    seg_beta,
    allowed,
):
    devices = lax.axis_size(AXES)
    n_beta = vector.shape[1]
    n_alpha, pairs = alpha_addr.shape
    mine = n_alpha // 2
    side = LANES // (2 * integrals.shape[0])
    rows, head = start(vector, integrals, devices)
    vec = lax.all_to_all(
        rows, AXES, split_axis=0, concat_axis=0, tiled=True
    ).reshape(n_alpha, 1, n_beta)
    tables = (alpha_addr, alpha_sign, seg_alpha.reshape(1, -1), seg_beta.reshape(1, -1), allowed)
    own, hot, mask = transform(
        integrals, head, orbitals, tables, (side, mine // side * n_alpha, pairs), (2, mine, n_beta)
    )
    partial = beta_side(vec, own, hot, mask, beta_addr, beta_sign, devices)
    parts = lax.all_to_all(partial, AXES, split_axis=0, concat_axis=0, tiled=True)
    return pl.pallas_call(
        add_kernel,
        out_shape=jax.ShapeDtypeStruct((n_beta // devices, n_alpha), jnp.float32),
        compiler_params=pltpu.CompilerParams(vmem_limit_bytes=VMEM_LIMIT),
        name="add_parts",
    )(parts)


def solution(mesh):
    rows = P(AXES, None)
    placed = (rows, P(AXES, None, None), P(), P(), P(), P(), P(), P(), P(), P())
    return jax.shard_map(on_device, mesh=mesh, in_specs=placed, out_specs=rows, check_vma=False)
```

profile of v0, /device:TPU:0, one launch (start us, length us, event | category | flops | bytes accessed | tf_op | source)
XLA Modules:
  0.0 36.3 jit_solution(7726453492181007728)
XLA Ops:
  0.0 1.4 %start.1 = (bf16[32,1,128]{2,1,0:T(2,128)(2,1)S(1)}, bf16[2,25,32,500]{3,2,1,0:T(8,128)(2,1)S(1)}) custom-call(bf16[1,128]{1,0:T(2,128)(2,1)} %vector_any.1, bf16[500,32,500]{2,1,0:T(8,128)(2,1)} %bitcast.13), custom_call_target="tpu_custom_call" | custom-call | tf_op jit(solution)/shard_map/start/pallas_call | solution.py:86
  1.4 0.0 copy-start
  1.5 0.0 copy-start.1
  1.5 7.8 %transform.1 = (bf16[32,676]{1,0:T(8,128)(2,1)S(1)}, bf16[2,256,676]{2,1,0:T(8,128)(2,1)S(1)}, f32[2,16,128]{2,1,0:T(8,128)S(1)}) custom-call(bf16[500,32,500]{2,1,0:T(8,128)(2,1)} %bitcast.14, bf16[2,25,32,500]{3,2,1,0:T(8,128)(2,1)S(1)} %get-tuple-element.10.head_ref, bf16[26,500]{1,0:T(8,128)(2,1)} %orb_any.1, s32[32,676]{1,0:T(8,128)} %addr_any.1, ...), custom_call_target="tpu_custom_call" | custom-call | flops 4096000000 | bytes 16000000 | tf_op jit(solution)/shard_map/transform/pallas_call | solution.py:264
  9.3 0.5 %collective-permute-start = (bf16[32,676]{1,0:T(8,128)(2,1)S(1)}, bf16[32,676]{1,0:T(8,128)(2,1)S(1)}, u32[]{:S(2)}, u32[]{:S(2)}) collective-permute-start(bf16[32,676]{1,0:T(8,128)(2,1)S(1)} %get-tuple-element.11.own_ref), channel_id=1, source_target_pairs={{0,8},{8,0},{16,24},{24,16},{1,9},{9,1},{17,25},{25,17},{2,10},{10... | collective-permute-start | bytes 129800 | tf_op jit(solution)/shard_map/ppermute | solution.py:435
  9.8 13.9 %all_to_all.16.vec_ref = bf16[32,1,128]{2,1,0:T(2,128)(2,1)S(1)} all-to-all(bf16[32,1,128]{2,1,0:T(2,128)(2,1)S(1)} %get-tuple-element.14), channel_id=1, replica_groups=mesh['grp'=4,'blk'=8] {'grp','blk'}, dimensions={0} | all-to-all | bytes 16384 | tf_op jit(solution)/shard_map/all_to_all | solution.py:493
  23.7 0.0 copy-done
  23.7 0.0 copy-done.1
  23.7 1.9 %gather.1.pairs_ref = bf16[676,2048]{1,0:T(8,128)(2,1)S(1)} custom-call(bf16[32,1,128]{2,1,0:T(2,128)(2,1)S(1)} %all_to_all.16.vec_ref, f32[2,16,128]{2,1,0:T(8,128)S(1)} %get-tuple-element.13.mask_ref, s32[676,128]{1,0:T(8,128)S(1)} %bitcast.9, s32[676,128]{1,0:T(8,128)S(1)} %bitcast.10), custom_call_target="tpu_custom_call" | custom-call | bytes 11075584 | tf_op jit(solution)/shard_map/gather/pallas_call | solution.py:448
  25.6 0.0 collective-permute-done.other_ref
  25.6 1.2 %contract.1 = f32[32,128]{1,0:T(8,128)S(1)} custom-call(bf16[32,676]{1,0:T(8,128)(2,1)S(1)} %get-tuple-element.11.own_ref, bf16[32,676]{1,0:T(8,128)(2,1)S(1)} %collective-permute-done.other_ref, bf16[2,256,676]{2,1,0:T(8,128)(2,1)S(1)} %get-tuple-element.12.hot_ref, f32[2,16,128]{2,1,0:T(8,128)S(1)} %get-tuple-element.13.mask_ref, ...), custom_call_target="tpu_custom_call" | custom-call | tf_op jit(solution)/shard_map/contract/pallas_call | solution.py:456
  26.8 8.8 %all_to_all.17 = f32[32,1,128]{2,1,0:T(1,128)S(1)} all-to-all(f32[32,1,128]{2,1,0:T(1,128)S(1)} %bitcast.11), channel_id=1, replica_groups=mesh['grp'=4,'blk'=8] {'grp','blk'}, dimensions={0} | all-to-all | bytes 32768 | tf_op jit(solution)/shard_map/all_to_all | solution.py:501
  35.6 0.7 %add_parts.1 = f32[4,32]{1,0:T(4,128)} custom-call(f32[32,128]{1,0:T(8,128)S(1)} %bitcast.12), custom_call_target="tpu_custom_call" | custom-call | tf_op jit(solution)/shard_map/add_parts/pallas_call | solution.py:502
Async XLA Ops:
  1.4 22.3 %copy-start = (s32[128,676]{0,1:T(8,128)S(1)}, s32[128,676]{0,1:T(8,128)}, u32[]{:S(2)}) copy-start(s32[128,676]{0,1:T(8,128)} %param.15) | copy-start | bytes 1038340
  1.5 22.3 %copy-start.1 = (s32[128,676]{0,1:T(8,128)S(1)}, s32[128,676]{0,1:T(8,128)}, u32[]{:S(2)}) copy-start(s32[128,676]{0,1:T(8,128)} %param.16) | copy-start | bytes 1038340
  9.3 16.4 %collective-permute-start = (bf16[32,676]{1,0:T(8,128)(2,1)S(1)}, bf16[32,676]{1,0:T(8,128)(2,1)S(1)}, u32[]{:S(2)}, u32[]{:S(2)}) collective-permute-start(bf16[32,676]{1,0:T(8,128)(2,1)S(1)} %get-tuple-element.11.own_ref), channel_id=1, source_target_pairs={{0,8},{8,0},{16,24},{24,16},{1,9},{9,1},{17,25},{25,17},{2,10},{10... | collective-permute-start | bytes 129800 | tf_op jit(solution)/shard_map/ppermute | solution.py:435
where the time goes:
time: 36.5 us; the launch traced here: 36.3 us
  blocking collectives  22.7 us (62%)
  Pallas kernels  12.9 us (35%)
  starting transfers between devices  0.55 us (2%)
    all_to_all x1, blocking collectives, on_device(): lax.all_to_all(rows, AXES, split_axis=0, concat_axis=0, tiled=True)  13.9 us
    all_to_all x1, blocking collectives, on_device(): lax.all_to_all(partial, AXES, split_axis=0, concat_axis=0, tiled=True)  8.84 us
    pallas_call x1, Pallas kernels, transform(): pl.pallas_call(functools.partial(transform_kernel, sizes=sizes, half=half...  7.78 us
    pallas_call x1, Pallas kernels, beta_side(): pl.pallas_call(gather_kernel, out_shape=product, scratch_shapes=[source],...  1.9 us
    pallas_call x1, Pallas kernels, start(): pl.pallas_call(start_kernel, in_specs=[hbm] * 2, out_specs=(hbm, pl.Block...  1.44 us
    pallas_call x1, Pallas kernels, beta_side(): pl.pallas_call(contract_kernel, out_shape=made, scratch_shapes=sums, comp...  1.16 us
  transfers between devices with their start and end apart: 1, of which 0 were waited for; matrix products, arithmetic and copies ran while one was open for 0% of the time, Pallas kernels for 5%

commit v1 on v0

--- a/solution.py
+++ b/solution.py
@@ -12,7 +12,7 @@
 LANES = 128
 SUBLANES = 8
 PACK = 16
-UNROLL = 672
+UNROLL = 1344
 AHEAD = 3
 HEAD = 25
 BLOCK = 50
@@ -109,6 +109,8 @@
 def transform_kernel(
     big_ref,
     head_ref,
+    b_addr_any,
+    b_sign_any,
     orb_any,
     addr_any,
     sign_any,
@@ -118,6 +120,8 @@
     out_ref,
     hot_ref,
     mask_ref,
+    b_addr_ref,
+    b_sign_ref,
     block_ref,
     orb_ref,
     addr_ref,
@@ -129,6 +133,7 @@
     turn_ref,
     big_sem,
     small_sem,
+    table_sem,
     *,
     sizes,
     half,
@@ -164,12 +169,19 @@
     ]
     for copy in small:
         copy.start()
+    late = [
+        pltpu.make_async_copy(b_addr_any, b_addr_ref, table_sem.at[0]),
+        pltpu.make_async_copy(b_sign_any, b_sign_ref, table_sem.at[1]),
+    ]
     for s in range(1, 1 + AHEAD):
         for copy in fetch(s):
             copy.start()
     small[0].wait()
     weights = orb_ref[...]
     for s, size in enumerate(sizes):
+        if s == len(sizes) - 1:
+            for copy in late:
+                copy.start()
         source, begin = (block_ref, starts[s] - first) if s else (head_ref, 0)
         for copy in fetch(s) if s else ():
             copy.wait()
@@ -207,6 +219,8 @@
         sums = jnp.dot(both, right, preferred_element_type=jnp.float32)
         turn_ref[pl.ds(r, norb, stride=PACK), :] = sums[:norb] + pltpu.roll(sums[32 : 32 + norb], LANES - groups * 32, 1)
     flatten(turn_ref, out_ref, norb, groups)
+    for copy in late:
+        copy.wait()
 
 
 def flatten(turn_ref, out_ref, norb, groups):
@@ -238,7 +252,7 @@
             )
 
 
-def transform(integrals, head, orbitals, tables, hot_shape, mask_shape):
+def transform(integrals, head, orbitals, tables, hot_shape, mask_shape, beta):
     aux, nbas, _ = integrals.shape
     norb = orbitals.shape[0]
     half = nbas // 2
@@ -252,7 +266,7 @@
             .reshape(aux, norb * norb)
             .astype(jnp.bfloat16)
         )
-        return factors, *pl.pallas_call(prepare, out_shape=made, name="prepare")(*tables)
+        return factors, *pl.pallas_call(prepare, out_shape=made, name="prepare")(*tables), *beta
     sizes = (head.shape[1],) + block_sizes(half - head.shape[1])
     stride = -(-half // 4) * 4
     stride += 4 if stride % SUBLANES == 0 else 0
@@ -261,10 +275,13 @@
     turned, orbitals, *tables = (
         pltpu.with_memory_space_constraint(t, pltpu.HBM) for t in (turned, orbitals, *tables)
     )
+    beta = [pltpu.with_memory_space_constraint(t, pltpu.HBM) for t in beta]
     return pl.pallas_call(
         functools.partial(transform_kernel, sizes=sizes, half=half, stride=stride),
-        in_specs=[hbm, pl.BlockSpec(memory_space=pltpu.VMEM)] + [hbm] * (1 + len(tables)),
-        out_shape=(jax.ShapeDtypeStruct((aux, norb * norb), jnp.bfloat16),) + made,
+        in_specs=[hbm, pl.BlockSpec(memory_space=pltpu.VMEM)] + [hbm] * (3 + len(tables)),
+        out_shape=(jax.ShapeDtypeStruct((aux, norb * norb), jnp.bfloat16),)
+        + made
+        + tuple(jax.ShapeDtypeStruct(t.shape, t.dtype) for t in beta),
         scratch_shapes=[
             pltpu.VMEM((2, half - sizes[0], aux, nbas), jnp.bfloat16),
             pltpu.VMEM(orbitals.shape, orbitals.dtype),
@@ -275,13 +292,14 @@
             pltpu.VMEM((norb * PACK, LANES), jnp.float32),
             pltpu.SemaphoreType.DMA((len(sizes), 2)),
             pltpu.SemaphoreType.DMA((1 + len(tables),)),
+            pltpu.SemaphoreType.DMA((2,)),
         ],
         cost_estimate=pl.CostEstimate(
             flops=4 * aux * nbas * nbas * LANES, transcendentals=0, bytes_accessed=2 * aux * nbas * nbas
         ),
         compiler_params=pltpu.CompilerParams(vmem_limit_bytes=WIDE_LIMIT),
         name="transform",
-    )(turned, head, orbitals, *tables)
+    )(turned, head, *beta, orbitals, *tables)
 
 
 def block_sizes(rows):
@@ -428,12 +446,11 @@
     finish(h_ref, t_ref, mask_ref, turn_ref, out_ref)
 
 
-def beta_side(vec, own, hot, mask, beta_addr, beta_sign, devices):
+def beta_side(vec, own, hot, mask, addr, sign, devices):
     aux, pairs = own.shape
     halves, mine, n_beta = mask.shape
     groups = lax.axis_size("grp")
     other = lax.ppermute(own, "grp", [(g, g ^ 1) for g in range(groups)])
-    addr, sign = beta_addr.T, beta_sign.T
     held = max(k for k in range(1, mine + 1) if mine % k == 0 and k * pairs * n_beta * 2 <= 12 * 2**20)
     params = pltpu.CompilerParams(vmem_limit_bytes=VMEM_LIMIT)
     made = jax.ShapeDtypeStruct((devices, n_beta // devices * halves * mine), jnp.float32)
@@ -494,10 +511,10 @@
         rows, AXES, split_axis=0, concat_axis=0, tiled=True
     ).reshape(n_alpha, 1, n_beta)
     tables = (alpha_addr, alpha_sign, seg_alpha.reshape(1, -1), seg_beta.reshape(1, -1), allowed)
-    own, hot, mask = transform(
-        integrals, head, orbitals, tables, (side, mine // side * n_alpha, pairs), (2, mine, n_beta)
-    )
-    partial = beta_side(vec, own, hot, mask, beta_addr, beta_sign, devices)
+    own, hot, mask, addr, sign = transform(
+        integrals, head, orbitals, tables, (side, mine // side * n_alpha, pairs), (2, mine, n_beta), (beta_addr.T, beta_sign.T)
+    )
+    partial = beta_side(vec, own, hot, mask, addr, sign, devices)
     parts = lax.all_to_all(partial, AXES, split_axis=0, concat_axis=0, tiled=True)
     return pl.pallas_call(
         add_kernel,

time: 36.5 us -> 36.3 us (level)
  no operation moved by 1% of the time
where the time goes in v1:
time: 36.3 us; the launch traced here: 36.1 us
  blocking collectives  22.7 us (63%)
  Pallas kernels  12.8 us (35%)
  starting transfers between devices  0.55 us (2%)
    all_to_all x1, blocking collectives, on_device(): lax.all_to_all(rows, AXES, split_axis=0, concat_axis=0, tiled=True)  13.9 us
    all_to_all x1, blocking collectives, on_device(): lax.all_to_all(partial, AXES, split_axis=0, concat_axis=0, tiled=True)  8.84 us
    pallas_call x1, Pallas kernels, transform(): pl.pallas_call(functools.partial(transform_kernel, sizes=sizes, half=half...  7.78 us
    pallas_call x1, Pallas kernels, beta_side(): pl.pallas_call(gather_kernel, out_shape=product, scratch_shapes=[source],...  1.78 us
    pallas_call x1, Pallas kernels, start(): pl.pallas_call(start_kernel, in_specs=[hbm] * 2, out_specs=(hbm, pl.Block...  1.44 us
    pallas_call x1, Pallas kernels, beta_side(): pl.pallas_call(contract_kernel, out_shape=made, scratch_shapes=sums, comp...  1.15 us
  transfers between devices with their start and end apart: 1, of which 0 were waited for; matrix products, arithmetic and copies ran while one was open for 0% of the time, Pallas kernels for 5%

profile of v1, /device:TPU:0, one launch (start us, length us, event | category | flops | bytes accessed | tf_op | source)
XLA Modules:
  0.0 36.1 jit_solution(12225500517616398654)
XLA Ops:
  0.0 1.4 %start.1 = (bf16[32,1,128]{2,1,0:T(2,128)(2,1)S(1)}, bf16[2,25,32,500]{3,2,1,0:T(8,128)(2,1)S(1)}) custom-call(bf16[1,128]{1,0:T(2,128)(2,1)} %vector_any.1, bf16[500,32,500]{2,1,0:T(8,128)(2,1)} %bitcast.11), custom_call_target="tpu_custom_call" | custom-call | tf_op jit(solution)/shard_map/start/pallas_call | solution.py:86
  1.4 7.8 %transform.1 = (bf16[32,676]{1,0:T(8,128)(2,1)S(1)}, bf16[2,256,676]{2,1,0:T(8,128)(2,1)S(1)}, f32[2,16,128]{2,1,0:T(8,128)S(1)}, s32[676,128]{1,0:T(8,128)S(1)}, s32[676,128]{1,0:T(8,128)S(1)}) custom-call(bf16[500,32,500]{2,1,0:T(8,128)(2,1)} %bitcast.12, bf16[2,25,32,500]{3,2,1,0:T(8,128)(2,1)S(1)} %get-tuple-element.12.head_ref, s32[676,128]{1,0:T(8,128)} %bitcast.13, ...), custom_call_target="tpu_custom_call" | custom-call | flops 4096000000 | bytes 16000000 | tf_op jit(solution)/shard_map/transform/pallas_call | solution.py:279
  9.2 0.6 %collective-permute-start = (bf16[32,676]{1,0:T(8,128)(2,1)S(1)}, bf16[32,676]{1,0:T(8,128)(2,1)S(1)}, u32[]{:S(2)}, u32[]{:S(2)}) collective-permute-start(bf16[32,676]{1,0:T(8,128)(2,1)S(1)} %get-tuple-element.13.own_ref), channel_id=1, source_target_pairs={{0,8},{8,0},{16,24},{24,16},{1,9},{9,1},{17,25},{25,17},{2,10},{10... | collective-permute-start | bytes 129800 | tf_op jit(solution)/shard_map/ppermute | solution.py:453
  9.8 13.9 %all_to_all.16.vec_ref = bf16[32,1,128]{2,1,0:T(2,128)(2,1)S(1)} all-to-all(bf16[32,1,128]{2,1,0:T(2,128)(2,1)S(1)} %get-tuple-element.16), channel_id=1, replica_groups=mesh['grp'=4,'blk'=8] {'grp','blk'}, dimensions={0} | all-to-all | bytes 16384 | tf_op jit(solution)/shard_map/all_to_all | solution.py:510
  23.7 1.8 %gather.1.pairs_ref = bf16[676,2048]{1,0:T(8,128)(2,1)S(1)} custom-call(bf16[32,1,128]{2,1,0:T(2,128)(2,1)S(1)} %all_to_all.16.vec_ref, f32[2,16,128]{2,1,0:T(8,128)S(1)} %get-tuple-element.15.mask_ref, s32[676,128]{1,0:T(8,128)S(1)} %get-tuple-element.17.addr_ref, s32[676,128]{1,0:T(8,128)S(1)} %get-tuple-element.18.sign_ref), custom_call_target="tpu_custom_call" | custom-call | bytes 11075584 | tf_op jit(solution)/shard_map/gather/pallas_call | solution.py:465
  25.4 0.0 collective-permute-done.other_ref
  25.5 1.2 %contract.1 = f32[32,128]{1,0:T(8,128)S(1)} custom-call(bf16[32,676]{1,0:T(8,128)(2,1)S(1)} %get-tuple-element.13.own_ref, bf16[32,676]{1,0:T(8,128)(2,1)S(1)} %collective-permute-done.other_ref, bf16[2,256,676]{2,1,0:T(8,128)(2,1)S(1)} %get-tuple-element.14.hot_ref, f32[2,16,128]{2,1,0:T(8,128)S(1)} %get-tuple-element.15.mask_ref, ...), custom_call_target="tpu_custom_call" | custom-call | tf_op jit(solution)/shard_map/contract/pallas_call | solution.py:473
  26.6 8.8 %all_to_all.17 = f32[32,1,128]{2,1,0:T(1,128)S(1)} all-to-all(f32[32,1,128]{2,1,0:T(1,128)S(1)} %bitcast.9), channel_id=1, replica_groups=mesh['grp'=4,'blk'=8] {'grp','blk'}, dimensions={0} | all-to-all | bytes 32768 | tf_op jit(solution)/shard_map/all_to_all | solution.py:518
  35.5 0.7 %add_parts.1 = f32[4,32]{1,0:T(4,128)} custom-call(f32[32,128]{1,0:T(8,128)S(1)} %bitcast.10), custom_call_target="tpu_custom_call" | custom-call | tf_op jit(solution)/shard_map/add_parts/pallas_call | solution.py:519
Async XLA Ops:
  9.2 16.2 %collective-permute-start = (bf16[32,676]{1,0:T(8,128)(2,1)S(1)}, bf16[32,676]{1,0:T(8,128)(2,1)S(1)}, u32[]{:S(2)}, u32[]{:S(2)}) collective-permute-start(bf16[32,676]{1,0:T(8,128)(2,1)S(1)} %get-tuple-element.13.own_ref), channel_id=1, source_target_pairs={{0,8},{8,0},{16,24},{24,16},{1,9},{9,1},{17,25},{25,17},{2,10},{10... | collective-permute-start | bytes 129800 | tf_op jit(solution)/shard_map/ppermute | solution.py:453

commit v2 on v1

--- a/solution.py
+++ b/solution.py
@@ -16,7 +16,7 @@
 AHEAD = 3
 HEAD = 25
 BLOCK = 50
-PREPARE_AT = 1
+PREPARE_AT = 2
 VMEM_LIMIT = 32 * 2**20
 WIDE_LIMIT = 50 * 2**20
 NT = (((1,), (1,)), ((), ()))
@@ -288,8 +288,8 @@
         ]
         + [pltpu.VMEM(t.shape, t.dtype) for t in tables]
         + [
-            pltpu.VMEM((PACK * stride, LANES), jnp.float32),
-            pltpu.VMEM((norb * PACK, LANES), jnp.float32),
+            pltpu.VMEM((PACK * stride + SUBLANES, LANES), jnp.float32),
+            pltpu.VMEM((-(-norb // SUBLANES) * SUBLANES * PACK, LANES), jnp.float32),
             pltpu.SemaphoreType.DMA((len(sizes), 2)),
             pltpu.SemaphoreType.DMA((1 + len(tables),)),
             pltpu.SemaphoreType.DMA((2,)),
@@ -455,7 +455,7 @@
     params = pltpu.CompilerParams(vmem_limit_bytes=VMEM_LIMIT)
     made = jax.ShapeDtypeStruct((devices, n_beta // devices * halves * mine), jnp.float32)
     source = pltpu.VMEM((mine // held, held, n_beta), jnp.float32)
-    product = jax.ShapeDtypeStruct((pairs, held * n_beta), jnp.bfloat16)
+    product = jax.ShapeDtypeStruct((-(-pairs // PACK) * PACK, held * n_beta), jnp.bfloat16)
     sums = [
         pltpu.VMEM((halves * mine, mine * 2 * aux), jnp.float32),
         pltpu.VMEM((mine // held, held * 2 * aux, n_beta), jnp.float32),

time: 36.3 us -> 36.1 us (level)
  no operation moved by 1% of the time
where the time goes in v2:
time: 36.1 us; the launch traced here: 35.9 us
  blocking collectives  22.7 us (63%)
  Pallas kernels  12.6 us (35%)
  starting transfers between devices  0.56 us (2%)
    all_to_all x1, blocking collectives, on_device(): lax.all_to_all(rows, AXES, split_axis=0, concat_axis=0, tiled=True)  13.9 us
    all_to_all x1, blocking collectives, on_device(): lax.all_to_all(partial, AXES, split_axis=0, concat_axis=0, tiled=True)  8.84 us
    pallas_call x1, Pallas kernels, transform(): pl.pallas_call(functools.partial(transform_kernel, sizes=sizes, half=half...  7.57 us
    pallas_call x1, Pallas kernels, beta_side(): pl.pallas_call(gather_kernel, out_shape=product, scratch_shapes=[source],...  1.78 us
    pallas_call x1, Pallas kernels, start(): pl.pallas_call(start_kernel, in_specs=[hbm] * 2, out_specs=(hbm, pl.Block...  1.44 us
    pallas_call x1, Pallas kernels, beta_side(): pl.pallas_call(contract_kernel, out_shape=made, scratch_shapes=sums, comp...  1.16 us
  transfers between devices with their start and end apart: 1, of which 0 were waited for; matrix products, arithmetic and copies ran while one was open for 0% of the time, Pallas kernels for 5%

profile of v2, /device:TPU:0, one launch (start us, length us, event | category | flops | bytes accessed | tf_op | source)
XLA Modules:
  0.0 35.9 jit_solution(2474672266576496208)
XLA Ops:
  0.0 1.4 %start.1 = (bf16[32,1,128]{2,1,0:T(2,128)(2,1)S(1)}, bf16[2,25,32,500]{3,2,1,0:T(8,128)(2,1)S(1)}) custom-call(bf16[1,128]{1,0:T(2,128)(2,1)} %vector_any.1, bf16[500,32,500]{2,1,0:T(8,128)(2,1)} %bitcast.11), custom_call_target="tpu_custom_call" | custom-call | tf_op jit(solution)/shard_map/start/pallas_call | solution.py:86
  1.4 7.6 %transform.1 = (bf16[32,676]{1,0:T(8,128)(2,1)S(1)}, bf16[2,256,676]{2,1,0:T(8,128)(2,1)S(1)}, f32[2,16,128]{2,1,0:T(8,128)S(1)}, s32[676,128]{1,0:T(8,128)S(1)}, s32[676,128]{1,0:T(8,128)S(1)}) custom-call(bf16[500,32,500]{2,1,0:T(8,128)(2,1)} %bitcast.12, bf16[2,25,32,500]{3,2,1,0:T(8,128)(2,1)S(1)} %get-tuple-element.12.head_ref, s32[676,128]{1,0:T(8,128)} %bitcast.13, ...), custom_call_target="tpu_custom_call" | custom-call | flops 4096000000 | bytes 16000000 | tf_op jit(solution)/shard_map/transform/pallas_call | solution.py:279
  9.0 0.6 %collective-permute-start = (bf16[32,676]{1,0:T(8,128)(2,1)S(1)}, bf16[32,676]{1,0:T(8,128)(2,1)S(1)}, u32[]{:S(2)}, u32[]{:S(2)}) collective-permute-start(bf16[32,676]{1,0:T(8,128)(2,1)S(1)} %get-tuple-element.13.own_ref), channel_id=1, source_target_pairs={{0,8},{8,0},{16,24},{24,16},{1,9},{9,1},{17,25},{25,17},{2,10},{10... | collective-permute-start | bytes 129800 | tf_op jit(solution)/shard_map/ppermute | solution.py:453
  9.6 13.9 %all_to_all.16.vec_ref = bf16[32,1,128]{2,1,0:T(2,128)(2,1)S(1)} all-to-all(bf16[32,1,128]{2,1,0:T(2,128)(2,1)S(1)} %get-tuple-element.16), channel_id=1, replica_groups=mesh['grp'=4,'blk'=8] {'grp','blk'}, dimensions={0} | all-to-all | bytes 16384 | tf_op jit(solution)/shard_map/all_to_all | solution.py:510
  23.5 1.8 %gather.1.pairs_ref = bf16[688,2048]{1,0:T(8,128)(2,1)S(1)} custom-call(bf16[32,1,128]{2,1,0:T(2,128)(2,1)S(1)} %all_to_all.16.vec_ref, f32[2,16,128]{2,1,0:T(8,128)S(1)} %get-tuple-element.15.mask_ref, s32[676,128]{1,0:T(8,128)S(1)} %get-tuple-element.17.addr_ref, s32[676,128]{1,0:T(8,128)S(1)} %get-tuple-element.18.sign_ref), custom_call_target="tpu_custom_call" | custom-call | bytes 11075584 | tf_op jit(solution)/shard_map/gather/pallas_call | solution.py:465
  25.3 0.0 collective-permute-done.other_ref
  25.3 1.2 %contract.1 = f32[32,128]{1,0:T(8,128)S(1)} custom-call(bf16[32,676]{1,0:T(8,128)(2,1)S(1)} %get-tuple-element.13.own_ref, bf16[32,676]{1,0:T(8,128)(2,1)S(1)} %collective-permute-done.other_ref, bf16[2,256,676]{2,1,0:T(8,128)(2,1)S(1)} %get-tuple-element.14.hot_ref, f32[2,16,128]{2,1,0:T(8,128)S(1)} %get-tuple-element.15.mask_ref, ...), custom_call_target="tpu_custom_call" | custom-call | tf_op jit(solution)/shard_map/contract/pallas_call | solution.py:473
  26.4 8.8 %all_to_all.17 = f32[32,1,128]{2,1,0:T(1,128)S(1)} all-to-all(f32[32,1,128]{2,1,0:T(1,128)S(1)} %bitcast.9), channel_id=1, replica_groups=mesh['grp'=4,'blk'=8] {'grp','blk'}, dimensions={0} | all-to-all | bytes 32768 | tf_op jit(solution)/shard_map/all_to_all | solution.py:518
  35.3 0.7 %add_parts.1 = f32[4,32]{1,0:T(4,128)} custom-call(f32[32,128]{1,0:T(8,128)S(1)} %bitcast.10), custom_call_target="tpu_custom_call" | custom-call | tf_op jit(solution)/shard_map/add_parts/pallas_call | solution.py:519
Async XLA Ops:
  9.0 16.2 %collective-permute-start = (bf16[32,676]{1,0:T(8,128)(2,1)S(1)}, bf16[32,676]{1,0:T(8,128)(2,1)S(1)}, u32[]{:S(2)}, u32[]{:S(2)}) collective-permute-start(bf16[32,676]{1,0:T(8,128)(2,1)S(1)} %get-tuple-element.13.own_ref), channel_id=1, source_target_pairs={{0,8},{8,0},{16,24},{24,16},{1,9},{9,1},{17,25},{25,17},{2,10},{10... | collective-permute-start | bytes 129800 | tf_op jit(solution)/shard_map/ppermute | solution.py:453
